TPU v7x, 32 devices: a whole 2x2x4 slice. The times are simulated.
32 devices in a mesh: dom: 8 (over z, x), rep: 4 (over y, core).
Axes of the slice: x: 2, y: 2, z: 4, core: 2. Of those that a mesh axis runs over, the one named last changes fastest.
Arguments:
- features: bfloat16 [65536, 128], P('dom'), may hold values from -6 to 6
- weight: bfloat16 [128, 256], replicated, may hold values from -0.5 to 0.5
- out_grad: bfloat16 [65536, 256], P(('dom', 'rep')), may hold values from -6 to 6
- send_rows: int32 [8, 8, 64], P('dom'), may hold values from 0 to 8191, as said below
- send_count: int32 [8, 8], P('dom'), may hold values from 0 to 64, as said below
- tile_target: int32 [8, 4, 256], P('dom', 'rep'), may hold values from 0 to 15, as said below
- tile_source: int32 [8, 4, 256], P('dom', 'rep'), may hold values from 0 to 67, as said below
- tile_weights: bfloat16 [8, 4, 256, 128, 128], P('dom', 'rep'), may hold values from -0.125 to 0.125
Outputs:
- activated: bfloat16 [65536, 256], P(('dom', 'rep'))
- feature_grad: bfloat16 [65536, 128], P(('dom', 'rep'))
- weight_grad: float32 [128, 256], replicated
Inputs may be any that keep to these rules, and one draw needn't show every extreme that they name: Within one list send_rows[o, d] the rows are distinct and increasing; entries at slots c >= send_count[o, d] are ignored. send_count[o, o] is 0. Every owner sends exactly 64 rows to some partition, and every partition receives exactly 64 rows from some owner. `tile_target`: pairs of target and source tiles may repeat. `tile_source`: every halo source tile (64 to 67) is named by some tile of every group.
All inputs are finite; a program needn't handle non-finite values.
Results may differ from a plain program's by a relative error of at most 0.006.
Values may be sent and summed in bfloat16 or wider, within the bound.
No kernel may reach another device: no remote copies, remote signals or barrier semaphores. Data moves between devices by JAX's collectives and lax.ppermute only.
A program may use at most 128 MiB of HBM per device.

v0:
```python
import jax
import jax.numpy as jnp
from jax import lax
from jax.sharding import PartitionSpec as P


def shards(
    features, weight, out_grad, send_rows, send_count, tile_target, tile_source, tile_weights
):
    feat = features.shape[1]
    tile = tile_weights.shape[-1]
    rows = send_rows[0]
    counts = send_count[0]
    width = rows.shape[1]
    valid = jnp.arange(width, dtype=jnp.int32)[None, :] < counts[:, None]
    outgoing = jnp.where(valid[:, :, None], features[rows], jnp.zeros((), jnp.bfloat16))
    halo = lax.all_to_all(outgoing, "dom", split_axis=0, concat_axis=0, tiled=True)
    sources = jnp.concatenate([features, halo.reshape(-1, feat)], axis=0)
    targets = tile_target[0, 0]
    anchors = tile_source[0, 0]
    values = tile_weights[0, 0]
    tgt_count = out_grad.shape[0] // tile
    src_count = sources.shape[0] // tile
    blocks = sources.reshape(src_count, tile, feat)[anchors]
    prods = jnp.einsum("tij,tjf->tif", values, blocks, preferred_element_type=jnp.float32)
    gathered = jax.ops.segment_sum(prods, targets, num_segments=tgt_count)
    gathered = gathered.reshape(-1, feat).astype(jnp.bfloat16)
    pre = jnp.dot(gathered, weight, preferred_element_type=jnp.float32)
    activated = jax.nn.silu(pre).astype(jnp.bfloat16)
    sigma = jax.nn.sigmoid(pre)
    slope = sigma * (1.0 + pre * (1.0 - sigma))
    pre_grad = (out_grad.astype(jnp.float32) * slope).astype(jnp.bfloat16)
    weight_part = jnp.dot(gathered.T, pre_grad, preferred_element_type=jnp.float32)
    weight_grad = lax.psum(weight_part, ("dom", "rep"))
    agg_grad = jnp.dot(pre_grad, weight.T, preferred_element_type=jnp.float32).astype(jnp.bfloat16)
    dblocks = agg_grad.reshape(tgt_count, tile, feat)[targets]
    backward = jnp.einsum("tij,tif->tjf", values, dblocks, preferred_element_type=jnp.float32)
    source_grad = jax.ops.segment_sum(backward, anchors, num_segments=src_count).reshape(-1, feat)
    owned_rows = features.shape[0]
    local = source_grad[:owned_rows]
    incoming = source_grad[owned_rows:].reshape(-1, width, feat)
    returned = lax.all_to_all(incoming, "dom", split_axis=0, concat_axis=0, tiled=True)
    kept = jnp.where(valid[:, :, None], returned, jnp.zeros((), jnp.float32))
    local = local.at[rows.reshape(-1)].add(kept.reshape(-1, feat))
    node_grad = lax.psum_scatter(local, "rep", scatter_dimension=0, tiled=True).astype(jnp.bfloat16)
    return (activated, node_grad, weight_grad)


def solution(mesh):
    return jax.shard_map(
        shards,
        mesh=mesh,
        in_specs=(
            P("dom", None),
            P(),
            P(("dom", "rep"), None),
            P("dom", None, None),
            P("dom", None),
            P("dom", "rep", None),
            P("dom", "rep", None),
            P("dom", "rep", None, None, None),
        ),
        out_specs=(P(("dom", "rep"), None), P(("dom", "rep"), None), P()),
        check_vma=False,
    )
```

profile of v0, /device:TPU:0, one launch (start us, length us, event | category | flops | bytes accessed | tf_op | source)
XLA Modules:
  0.0 379.2 jit_solution(14296807344320537851)
XLA Ops:
  8.0 0.0 copy-start
  8.0 0.8 iota_compare_fusion
  8.8 0.7 compare_select_fusion.1
  9.5 0.1 reshape.170
  9.6 2.9 gather_fusion
  12.5 0.8 broadcast_select_fusion.1
  13.3 7.3 %all-to-all-start = ((bf16[8,64,128]{2,1,0:T(8,128)(2,1)}), bf16[8,64,128]{2,1,0:T(8,128)(2,1)S(1)}, u32[]{:S(2)}, u32[]{:S(2)}) async-start(bf16[8,64,128]{2,1,0:T(8,128)(2,1)} %broadcast_select_fusion.1), calls=%async_computation | async-start | bytes 262144 | tf_op jit(solution)/shard_map/all_to_all | solution.py:17
  20.5 0.7 compare_select_fusion.3
  21.2 0.7 compare_select_fusion.2
  21.9 6.0 %all-to-all-done = bf16[8,64,128]{2,1,0:T(8,128)(2,1)S(1)} async-done(((bf16[8,64,128]{2,1,0:T(8,128)(2,1)}), bf16[8,64,128]{2,1,0:T(8,128)(2,1)S(1)}, u32[]{:S(2)}, u32[]{:S(2)}) %all-to-all-start) | async-done | bytes 131104 | tf_op jit(solution)/shard_map/all_to_all | solution.py:17
  27.9 5.3 %pad_maximum_fusion = bf16[8704,128]{1,0:T(8,128)(2,1)S(1)} fusion(bf16[512,128]{1,0:T(8,128)(2,1)S(1)} %bitcast.45, bf16[8192,128]{1,0:T(8,128)(2,1)} %param.8), kind=kLoop, calls=%fused_computation.11 | loop fusion | flops 4456448 | bytes 4456448 | tf_op jit(solution)/shard_map/concatenate | solution.py:18
  33.2 8.6 %gather_fusion.1 = bf16[256,128,128]{2,1,0:T(8,128)(2,1)} fusion(bf16[68,128,128]{2,1,0:T(8,128)(2,1)S(1)} %bitcast.40, s32[1024]{0:T(1024)S(1)} %pad_clamp_fusion.1), kind=kCustom, calls=%fused_computation.1 | custom fusion | bytes 16778240 | tf_op jit(solution)/shard_map/gather | solution.py:24
  41.9 12.8 %convolution_bitcast_fusion.1 = f32[256,128,128]{1,2,0:T(8,128)} fusion(bf16[256,128,128]{2,1,0:T(8,128)(2,1)} %gather_fusion.1, bf16[1,1,256,128,128]{4,3,2,1,0:T(8,128)(2,1)} %param.15), kind=kOutput, calls=%fused_computation.7 | convolution fusion | flops 1073741824 | bytes 33554432 | tf_op jit(solution)/shard_map/tij,tjf->tif/dot_general | solution.py:25
  54.7 0.0 copy-start.3
  54.7 17.5 %copy.14 = f32[256,128,128]{2,1,0:T(8,128)} copy(f32[256,128,128]{1,2,0:T(8,128)} %convolution_bitcast_fusion.1) | data formatting | bytes 33554432 | tf_op jit(solution)/shard_map/tij,tjf->tif/dot_general | solution.py:25
  72.2 0.1 broadcast_in_dim.35
  72.3 0.0 copy-done.3
  72.3 0.0 copy-start.5
  72.3 33.2 %scatter_fusion = f32[16,128,128]{2,1,0:T(8,128)S(1)} fusion(f32[16,128,128]{2,1,0:T(8,128)S(1)} %broadcast_in_dim.35, s32[256]{0:T(256)S(1)} %bitcast.48, f32[256,128,128]{2,1,0:T(8,128)} %copy.14), kind=kCustom, calls=%fused_computation.3 | custom fusion | flops 4194304 | bytes 50332672 | tf_op jit(solution)/shard_map/scatter-add | solution.py:26
  105.5 0.1 convert_element_type.21
  105.6 0.0 copy-done
  105.6 0.0 copy-done.5
  105.6 2.1 multiply_convert_fusion
  107.7 0.4 convolution_convert_fusion
  108.1 8.8 %gather_fusion.2 = bf16[256,128,128]{2,1,0:T(8,128)(2,1)} fusion(bf16[16,128,128]{2,1,0:T(8,128)(2,1)S(1)} %bitcast.39, s32[1024]{0:T(1024)S(1)} %pad_clamp_fusion), kind=kCustom, calls=%fused_computation.2 | custom fusion | bytes 16778240 | tf_op jit(solution)/shard_map/gather | solution.py:36
  116.9 14.4 %convolution_bitcast_fusion = f32[256,128,128]{1,2,0:T(8,128)} fusion(bf16[256,128,128]{2,1,0:T(8,128)(2,1)} %gather_fusion.2, bf16[1,1,256,128,128]{4,3,2,1,0:T(8,128)(2,1)} %param.15), kind=kOutput, calls=%fused_computation.6 | convolution fusion | flops 1073741824 | bytes 33554432 | tf_op jit(solution)/shard_map/tij,tif->tjf/dot_general | solution.py:37
  131.3 17.5 %copy.16 = f32[256,128,128]{2,1,0:T(8,128)} copy(f32[256,128,128]{1,2,0:T(8,128)} %convolution_bitcast_fusion) | data formatting | bytes 33554432 | tf_op jit(solution)/shard_map/tij,tif->tjf/dot_general | solution.py:37
  148.8 2.6 broadcast_in_dim.38
  151.3 0.0 copy-done.4
  151.3 51.9 %scatter_fusion.1 = f32[68,128,128]{2,1,0:T(8,128)} fusion(f32[68,128,128]{2,1,0:T(8,128)} %broadcast_in_dim.38, s32[256]{0:T(256)S(1)} %bitcast.49, f32[256,128,128]{2,1,0:T(8,128)} %copy.16), kind=kCustom, calls=%fused_computation.4 | custom fusion | flops 4194304 | bytes 50332672 | tf_op jit(solution)/shard_map/scatter-add | solution.py:38
  203.2 1.7 slice.20
  204.9 3.4 all-to-all-start.1
  208.3 0.0 reduce-scatter.2.cloned.1.call-start
  208.3 0.0 copy-done.2
  208.4 0.1 reshape_squeeze.3
  208.4 4.7 %slice.19 = f32[64,128,128]{2,1,0:T(8,128)} slice(f32[68,128,128]{2,1,0:T(8,128)} %scatter_fusion.1), slice={[0:64], [0:128], [0:128]} | slice | bytes 8388608 | tf_op jit(solution)/shard_map/slice | solution.py:40
  213.1 3.4 all-to-all-done.1
  216.5 0.1 broadcast_select_fusion
  216.6 7.1 %scatter_fusion.2 = f32[8192,128]{1,0:T(8,128)} fusion(f32[8192,128]{1,0:T(8,128)} %bitcast.41, s32[512]{0:T(512)S(1)} %bitcast.47, f32[512,128]{1,0:T(8,128)S(1)} %bitcast.44), kind=kCustom, calls=%fused_computation.5 | custom fusion | flops 65536 | bytes 788480 | tf_op jit(solution)/shard_map/scatter-add | solution.py:44
  223.8 0.0 reduce-scatter.2.cloned.1.call-update
  223.8 0.0 all-reduce.2.cloned.1.call-start
  223.8 1.0 fusion.2
  224.8 0.0 all-reduce.2.cloned.1.call-update
  224.9 42.1 %reduce-scatter.2.cloned.1.call-done = f32[2048,128]{1,0:T(8,128)} async-done(((f32[8192,128]{1,0:T(8,128)}), f32[2048,128]{1,0:T(8,128)}) %reduce-scatter.2.cloned.1.call-update) | async-done | bytes 1048592 | tf_op jit(solution)/shard_map/reduce_scatter | solution.py:45
  267.0 2.1 convert_element_type.27
  269.1 101.1 %all-reduce.2.cloned.1.call-done = f32[128,256]{1,0:T(8,128)} async-done(((f32[128,256]{1,0:T(8,128)}), f32[128,256]{1,0:T(8,128)}) %all-reduce.2.cloned.1.call-update) | async-done | bytes 131088 | tf_op jit(solution)/shard_map/psum | solution.py:34
  370.2 1.6 copy.23
  371.7 0.0 copy-done.1
  (7 shorter events, 0.0 us)
Async XLA Ops:
  8.0 97.6 %copy-start = (bf16[128,256]{1,0:T(8,128)(2,1)S(1)}, bf16[128,256]{1,0:T(8,128)(2,1)}, u32[]{:S(2)}) copy-start(bf16[128,256]{1,0:T(8,128)(2,1)} %param.9) | copy-start | bytes 196612
  13.3 14.6 %all-to-all-start = ((bf16[8,64,128]{2,1,0:T(8,128)(2,1)}), bf16[8,64,128]{2,1,0:T(8,128)(2,1)S(1)}, u32[]{:S(2)}, u32[]{:S(2)}) async-start(bf16[8,64,128]{2,1,0:T(8,128)(2,1)} %broadcast_select_fusion.1), calls=%async_computation | async-start | bytes 262144 | tf_op jit(solution)/shard_map/all_to_all | solution.py:17
  54.7 17.6 %copy-start.3 = (s32[1,1,256]{2,1,0:T(1,128)S(1)}, s32[1,1,256]{2,1,0:T(1,128)}, u32[]{:S(2)}) copy-start(s32[1,1,256]{2,1,0:T(1,128)} %param.13) | copy-start | bytes 3076
  72.3 33.3 %copy-start.5 = (bf16[2048,256]{1,0:T(8,128)(2,1)S(1)}, bf16[2048,256]{1,0:T(8,128)(2,1)}, u32[]{:S(2)}) copy-start(bf16[2048,256]{1,0:T(8,128)(2,1)} %param.10) | copy-start | bytes 3145732
  131.3 20.0 %copy-start.4 = (s32[1,1,256]{2,1,0:T(1,128)S(1)}, s32[1,1,256]{2,1,0:T(1,128)}, u32[]{:S(2)}) copy-start(s32[1,1,256]{2,1,0:T(1,128)} %param.14) | copy-start | bytes 3076
  151.3 57.0 %copy-start.2 = (s32[1,8,64]{2,1,0:T(8,128)S(1)}, s32[1,8,64]{2,1,0:T(8,128)}, u32[]{:S(2)}) copy-start(s32[1,8,64]{2,1,0:T(8,128)} %param.11) | copy-start | bytes 6148
  204.9 11.6 %all-to-all-start.1 = ((f32[8,64,128]{2,1,0:T(8,128)}), f32[8,64,128]{2,1,0:T(8,128)S(1)}, u32[]{:S(2)}, u32[]{:S(2)}) async-start(f32[8,64,128]{2,1,0:T(8,128)} %bitcast.18), calls=%async_computation.1 | async-start | bytes 524288 | tf_op jit(solution)/shard_map/all_to_all | solution.py:42
  208.3 58.7 %reduce-scatter.2.cloned.1.call-start = ((), (), s32[]{:S(2)}) async-start(), calls=%async_computation.3 | async-start | bytes 5242880 | tf_op jit(solution)/shard_map/reduce_scatter | solution.py:45
  208.4 163.3 %copy-start.1 = (bf16[128,256]{1,0:T(8,128)(2,1)S(1)}, bf16[128,256]{1,0:T(8,128)(2,1)}, u32[]{:S(2)}) copy-start(bf16[128,256]{1,0:T(8,128)(2,1)} %param.9) | copy-start | bytes 196612
  223.8 146.4 %all-reduce.2.cloned.1.call-start = ((), (), s32[]{:S(2)}) async-start(), calls=%async_computation.4 | async-start | bytes 262144 | tf_op jit(solution)/shard_map/psum | solution.py:34
Sparse Core Ops, SparseCore 0:
  223.9 43.0 reduce-scatter.1
Sparse Core Ops, SparseCore 1:
  230.4 139.7 all-reduce.1
where the time goes:
time: 381 us; the launch traced here: 379 us
  waiting for transfers between devices  153 us (40%)
  other arithmetic  103 us (27%)
  local copies, waits for them, and re-layouts  66 us (17%)
  matrix products  30.7 us (8%)
  between operations  15.6 us (4%)
  starting transfers between devices  10.8 us (3%)
    psum x1, waiting for transfers between devices, shards(): weight_grad = lax.psum(weight_part, ('dom', 'rep'))  101 us
    scatter-add x1, other arithmetic, shards(): jax.ops.segment_sum(backward, anchors, num_segments=src_count)  51.9 us
    reduce_scatter x1, waiting for transfers between devices, shards(): lax.psum_scatter(local, 'rep', scatter_dimension=0, tiled=True)  42.1 us
    scatter-add x1, other arithmetic, shards(): gathered = jax.ops.segment_sum(prods, targets, num_segments=tgt_count)  33.2 us
    dot_general x1, local copies, waits for them, and re-layouts, shards(): jnp.einsum('tij,tjf->tif', values, blocks, preferred_element_type=jnp.flo...  17.5 us
    dot_general x1, local copies, waits for them, and re-layouts, shards(): jnp.einsum('tij,tif->tjf', values, dblocks, preferred_element_type=jnp.fl...  17.5 us
    dot_general x1, matrix products, shards(): jnp.einsum('tij,tif->tjf', values, dblocks, preferred_element_type=jnp.fl...  14.4 us
    dot_general x1, matrix products, shards(): jnp.einsum('tij,tjf->tif', values, blocks, preferred_element_type=jnp.flo...  12.8 us
  transfers between devices with their start and end apart: 4, of which 4 were waited for; matrix products, arithmetic and copies ran while one was open for 2% of the time, Pallas kernels for 0%

commit v1 on v0

--- a/solution.py
+++ b/solution.py
@@ -31,7 +31,8 @@
     slope = sigma * (1.0 + pre * (1.0 - sigma))
     pre_grad = (out_grad.astype(jnp.float32) * slope).astype(jnp.bfloat16)
     weight_part = jnp.dot(gathered.T, pre_grad, preferred_element_type=jnp.float32)
-    weight_grad = lax.psum(weight_part, ("dom", "rep"))
+    _play_meshes = lambda unit: jax.lax.psum(jax.lax.psum(unit, "dom"), "rep")
+    weight_grad = _play_meshes(weight_part)
     agg_grad = jnp.dot(pre_grad, weight.T, preferred_element_type=jnp.float32).astype(jnp.bfloat16)
     dblocks = agg_grad.reshape(tgt_count, tile, feat)[targets]
     backward = jnp.einsum("tij,tif->tjf", values, dblocks, preferred_element_type=jnp.float32)

time: 381 us -> 328 us (0.86)
  waiting for transfers between devices: 153 us -> 98.5 us
    reduce_scatter x1, waiting for transfers between devices: 42.1 us -> 0.03 us  [shards(): lax.psum_scatter(local, 'rep', scatter_dimension=0, tiled=True)]
    psum x1 -> x2, waiting for transfers between devices: 101 us -> 90.9 us  [shards(): _play_meshes = lambda unit: jax.lax.psum(jax.lax.psum(unit, 'dom'), 'rep')]
  transfers between devices with their start and end apart: 4 -> 5, of which waited for: 4 -> 4; matrix products, arithmetic and copies ran while one was open for 2% -> 5% of each run, Pallas kernels for 0% -> 0%
where the time goes in v1:
time: 328 us; the launch traced here: 325 us
  other arithmetic  103 us (31%)
  waiting for transfers between devices  98.5 us (30%)
  local copies, waits for them, and re-layouts  66.7 us (20%)
  matrix products  30.7 us (9%)
  between operations  15.6 us (5%)
  starting transfers between devices  10.8 us (3%)
    psum x2, waiting for transfers between devices, shards(): _play_meshes = lambda unit: jax.lax.psum(jax.lax.psum(unit, 'dom'), 'rep')  90.9 us
    scatter-add x1, other arithmetic, shards(): jax.ops.segment_sum(backward, anchors, num_segments=src_count)  51.5 us
    scatter-add x1, other arithmetic, shards(): gathered = jax.ops.segment_sum(prods, targets, num_segments=tgt_count)  33.2 us
    dot_general x1, local copies, waits for them, and re-layouts, shards(): jnp.einsum('tij,tjf->tif', values, blocks, preferred_element_type=jnp.flo...  17.5 us
    dot_general x1, local copies, waits for them, and re-layouts, shards(): jnp.einsum('tij,tif->tjf', values, dblocks, preferred_element_type=jnp.fl...  17.5 us
    dot_general x1, matrix products, shards(): jnp.einsum('tij,tif->tjf', values, dblocks, preferred_element_type=jnp.fl...  14.4 us
    dot_general x1, matrix products, shards(): jnp.einsum('tij,tjf->tif', values, blocks, preferred_element_type=jnp.flo...  12.8 us
    gather x1, local copies, waits for them, and re-layouts, shards(): dblocks = agg_grad.reshape(tgt_count, tile, feat)[targets]  8.77 us
  transfers between devices with their start and end apart: 5, of which 4 were waited for; matrix products, arithmetic and copies ran while one was open for 5% of the time, Pallas kernels for 0%

profile of v1, /device:TPU:0, one launch (start us, length us, event | category | flops | bytes accessed | tf_op | source)
XLA Modules:
  0.0 325.4 jit_solution(9100214656433500407)
XLA Ops:
  8.0 0.0 copy-start
  8.0 0.8 iota_compare_fusion
  8.8 0.7 compare_select_fusion.1
  9.5 0.1 reshape.170
  9.6 2.9 gather_fusion
  12.5 0.8 broadcast_select_fusion.1
  13.3 7.3 %all-to-all-start = ((bf16[8,64,128]{2,1,0:T(8,128)(2,1)}), bf16[8,64,128]{2,1,0:T(8,128)(2,1)S(1)}, u32[]{:S(2)}, u32[]{:S(2)}) async-start(bf16[8,64,128]{2,1,0:T(8,128)(2,1)} %broadcast_select_fusion.1), calls=%async_computation | async-start | bytes 262144 | tf_op jit(solution)/shard_map/all_to_all | solution.py:17
  20.5 0.7 compare_select_fusion.3
  21.2 0.7 compare_select_fusion.2
  21.9 0.8 reshape_squeeze.3
  22.7 5.2 %all-to-all-done = bf16[8,64,128]{2,1,0:T(8,128)(2,1)S(1)} async-done(((bf16[8,64,128]{2,1,0:T(8,128)(2,1)}), bf16[8,64,128]{2,1,0:T(8,128)(2,1)S(1)}, u32[]{:S(2)}, u32[]{:S(2)}) %all-to-all-start) | async-done | bytes 131104 | tf_op jit(solution)/shard_map/all_to_all | solution.py:17
  27.9 5.3 %pad_maximum_fusion = bf16[8704,128]{1,0:T(8,128)(2,1)S(1)} fusion(bf16[512,128]{1,0:T(8,128)(2,1)S(1)} %bitcast.45, bf16[8192,128]{1,0:T(8,128)(2,1)} %param.8), kind=kLoop, calls=%fused_computation.11 | loop fusion | flops 4456448 | bytes 4456448 | tf_op jit(solution)/shard_map/concatenate | solution.py:18
  33.2 8.6 %gather_fusion.1 = bf16[256,128,128]{2,1,0:T(8,128)(2,1)} fusion(bf16[68,128,128]{2,1,0:T(8,128)(2,1)S(1)} %bitcast.40, s32[1024]{0:T(1024)S(1)} %pad_clamp_fusion.1), kind=kCustom, calls=%fused_computation.1 | custom fusion | bytes 16778240 | tf_op jit(solution)/shard_map/gather | solution.py:24
  41.8 12.8 %convolution_bitcast_fusion.1 = f32[256,128,128]{1,2,0:T(8,128)} fusion(bf16[256,128,128]{2,1,0:T(8,128)(2,1)} %gather_fusion.1, bf16[1,1,256,128,128]{4,3,2,1,0:T(8,128)(2,1)} %param.15), kind=kOutput, calls=%fused_computation.7 | convolution fusion | flops 1073741824 | bytes 33554432 | tf_op jit(solution)/shard_map/tij,tjf->tif/dot_general | solution.py:25
  54.7 17.5 %copy.14 = f32[256,128,128]{2,1,0:T(8,128)} copy(f32[256,128,128]{1,2,0:T(8,128)} %convolution_bitcast_fusion.1) | data formatting | bytes 33554432 | tf_op jit(solution)/shard_map/tij,tjf->tif/dot_general | solution.py:25
  72.2 0.1 broadcast_in_dim.35
  72.3 0.0 copy-done.2
  72.3 0.0 copy-start.4
  72.3 33.2 %scatter_fusion = f32[16,128,128]{2,1,0:T(8,128)S(1)} fusion(f32[16,128,128]{2,1,0:T(8,128)S(1)} %broadcast_in_dim.35, s32[256]{0:T(256)S(1)} %bitcast.48, f32[256,128,128]{2,1,0:T(8,128)} %copy.14), kind=kCustom, calls=%fused_computation.3 | custom fusion | flops 4194304 | bytes 50332672 | tf_op jit(solution)/shard_map/scatter-add | solution.py:26
  105.5 0.1 convert_element_type.21
  105.6 0.0 copy-done
  105.6 0.0 copy-done.4
  105.6 2.1 multiply_convert_fusion
  107.7 0.4 convolution_convert_fusion
  108.1 8.8 %gather_fusion.2 = bf16[256,128,128]{2,1,0:T(8,128)(2,1)} fusion(bf16[16,128,128]{2,1,0:T(8,128)(2,1)S(1)} %bitcast.39, s32[1024]{0:T(1024)S(1)} %pad_clamp_fusion), kind=kCustom, calls=%fused_computation.2 | custom fusion | bytes 16778240 | tf_op jit(solution)/shard_map/gather | solution.py:37
  116.9 14.4 %convolution_bitcast_fusion = f32[256,128,128]{1,2,0:T(8,128)} fusion(bf16[256,128,128]{2,1,0:T(8,128)(2,1)} %gather_fusion.2, bf16[1,1,256,128,128]{4,3,2,1,0:T(8,128)(2,1)} %param.15), kind=kOutput, calls=%fused_computation.6 | convolution fusion | flops 1073741824 | bytes 33554432 | tf_op jit(solution)/shard_map/tij,tif->tjf/dot_general | solution.py:38
  131.2 17.5 %copy.16 = f32[256,128,128]{2,1,0:T(8,128)} copy(f32[256,128,128]{1,2,0:T(8,128)} %convolution_bitcast_fusion) | data formatting | bytes 33554432 | tf_op jit(solution)/shard_map/tij,tif->tjf/dot_general | solution.py:38
  148.7 2.6 broadcast_in_dim.38
  151.3 51.5 %scatter_fusion.1 = f32[68,128,128]{2,1,0:T(8,128)} fusion(f32[68,128,128]{2,1,0:T(8,128)} %broadcast_in_dim.38, s32[256]{0:T(256)S(1)} %bitcast.49, f32[256,128,128]{2,1,0:T(8,128)} %copy.16), kind=kCustom, calls=%fused_computation.4 | custom fusion | flops 4194304 | bytes 50332672 | tf_op jit(solution)/shard_map/scatter-add | solution.py:39
  202.8 1.7 slice.20
  204.5 3.4 %all-to-all-start.1 = ((f32[8,64,128]{2,1,0:T(8,128)}), f32[8,64,128]{2,1,0:T(8,128)S(1)}, u32[]{:S(2)}, u32[]{:S(2)}) async-start(f32[8,64,128]{2,1,0:T(8,128)} %bitcast.18), calls=%async_computation.1 | async-start | bytes 524288 | tf_op jit(solution)/shard_map/all_to_all | solution.py:43
  207.9 0.0 all-reduce.3.cloned.1.call-start
  208.0 0.0 copy-start.1
  208.0 4.7 %slice.19 = f32[64,128,128]{2,1,0:T(8,128)} slice(f32[68,128,128]{2,1,0:T(8,128)} %scatter_fusion.1), slice={[0:64], [0:128], [0:128]} | slice | bytes 8388608 | tf_op jit(solution)/shard_map/slice | solution.py:41
  212.6 1.0 fusion.2
  213.6 0.0 all-reduce.3.cloned.1.call-update
  213.6 0.0 reduce-scatter.2.cloned.1.call-start
  213.7 2.4 all-to-all-done.1
  216.0 0.1 broadcast_select_fusion
  216.2 7.1 %scatter_fusion.2 = f32[8192,128]{1,0:T(8,128)} fusion(f32[8192,128]{1,0:T(8,128)} %bitcast.41, s32[512]{0:T(512)S(1)} %bitcast.47, f32[512,128]{1,0:T(8,128)S(1)} %bitcast.44), kind=kCustom, calls=%fused_computation.5 | custom fusion | flops 65536 | bytes 788480 | tf_op jit(solution)/shard_map/scatter-add | solution.py:45
  223.3 0.0 reduce-scatter.2.cloned.1.call-update
  223.3 0.0 all-reduce.5.cloned.1.call-start
  223.4 62.2 %all-reduce.3.cloned.1.call-done = f32[128,256]{1,0:T(8,128)} async-done(((f32[128,256]{1,0:T(8,128)}), f32[128,256]{1,0:T(8,128)}) %all-reduce.3.cloned.1.call-update) | async-done | bytes 131088 | tf_op jit(solution)/shard_map/psum | solution.py:34
  285.6 0.0 all-reduce.5.cloned.1.call-update
  285.6 0.0 reduce-scatter.2.cloned.1.call-done
  285.6 2.1 convert_element_type.27
  287.7 28.7 %all-reduce.5.cloned.1.call-done = f32[128,256]{1,0:T(8,128)} async-done(((f32[128,256]{1,0:T(8,128)}), f32[128,256]{1,0:T(8,128)}) %all-reduce.5.cloned.1.call-update) | async-done | bytes 131088 | tf_op jit(solution)/shard_map/psum | solution.py:34
  316.4 1.6 copy.24
  (8 shorter events, 0.0 us)
Async XLA Ops:
  8.0 97.6 %copy-start = (bf16[128,256]{1,0:T(8,128)(2,1)S(1)}, bf16[128,256]{1,0:T(8,128)(2,1)}, u32[]{:S(2)}) copy-start(bf16[128,256]{1,0:T(8,128)(2,1)} %param.9) | copy-start | bytes 196612
  13.3 14.6 %all-to-all-start = ((bf16[8,64,128]{2,1,0:T(8,128)(2,1)}), bf16[8,64,128]{2,1,0:T(8,128)(2,1)S(1)}, u32[]{:S(2)}, u32[]{:S(2)}) async-start(bf16[8,64,128]{2,1,0:T(8,128)(2,1)} %broadcast_select_fusion.1), calls=%async_computation | async-start | bytes 262144 | tf_op jit(solution)/shard_map/all_to_all | solution.py:17
  54.7 17.6 %copy-start.2 = (s32[1,1,256]{2,1,0:T(1,128)S(1)}, s32[1,1,256]{2,1,0:T(1,128)}, u32[]{:S(2)}) copy-start(s32[1,1,256]{2,1,0:T(1,128)} %param.13) | copy-start | bytes 3076
  72.3 33.3 %copy-start.4 = (bf16[2048,256]{1,0:T(8,128)(2,1)S(1)}, bf16[2048,256]{1,0:T(8,128)(2,1)}, u32[]{:S(2)}) copy-start(bf16[2048,256]{1,0:T(8,128)(2,1)} %param.10) | copy-start | bytes 3145732
  131.2 20.1 %copy-start.3 = (s32[1,1,256]{2,1,0:T(1,128)S(1)}, s32[1,1,256]{2,1,0:T(1,128)}, u32[]{:S(2)}) copy-start(s32[1,1,256]{2,1,0:T(1,128)} %param.14) | copy-start | bytes 3076
  204.5 11.6 %all-to-all-start.1 = ((f32[8,64,128]{2,1,0:T(8,128)}), f32[8,64,128]{2,1,0:T(8,128)S(1)}, u32[]{:S(2)}, u32[]{:S(2)}) async-start(f32[8,64,128]{2,1,0:T(8,128)} %bitcast.18), calls=%async_computation.1 | async-start | bytes 524288 | tf_op jit(solution)/shard_map/all_to_all | solution.py:43
  207.9 77.7 %all-reduce.3.cloned.1.call-start = ((), (), s32[]{:S(2)}) async-start(), calls=%async_computation.4 | async-start | bytes 262144 | tf_op jit(solution)/shard_map/psum | solution.py:34
  208.0 110.0 %copy-start.1 = (bf16[128,256]{1,0:T(8,128)(2,1)S(1)}, bf16[128,256]{1,0:T(8,128)(2,1)}, u32[]{:S(2)}) copy-start(bf16[128,256]{1,0:T(8,128)(2,1)} %param.9) | copy-start | bytes 196612
  213.6 72.0 %reduce-scatter.2.cloned.1.call-start = ((), (), s32[]{:S(2)}) async-start(), calls=%async_computation.3 | async-start | bytes 5242880 | tf_op jit(solution)/shard_map/reduce_scatter | solution.py:46
  223.3 93.1 %all-reduce.5.cloned.1.call-start = ((), (), s32[]{:S(2)}) async-start(), calls=%async_computation.5 | async-start | bytes 262144 | tf_op jit(solution)/shard_map/psum | solution.py:34
Sparse Core Ops, SparseCore 0:
  213.8 71.7 all-reduce.2
Sparse Core Ops, SparseCore 1:
  223.4 43.4 reduce-scatter.1
  285.7 30.6 all-reduce.4
